TPU v7x, 512 devices: a whole 4x4x16 slice. The times are simulated.
512 devices in a mesh: blk: 32 (over y_lo, z), gy: 4 (over x), rep: 4 (over y_hi, core).
Axes of the slice: x: 4, y: 4 (y_hi: 2, y_lo: 2; y = y_hi * 2 + y_lo), z: 16, core: 2. Of those that a mesh axis runs over, the one named last changes fastest.
Arguments:
- grain_id: int32 [128, 32, 512], P('blk', 'gy', 'rep'), may hold values from 0 to 255
- init_masks: int32 [2, 128, 32, 512], P(None, 'blk', 'gy', 'rep'), may hold values from 0 to 1, as said below
- target_masks: int32 [2, 128, 32, 512], P(None, 'blk', 'gy', 'rep'), may hold values from 0 to 1, as said below
- emb_table: bfloat16 [256, 8], replicated, may hold values from -6 to 6
- w_in: float32 [64, 10], P('rep'), may hold values from -2 to 2
- b_in: float32 [64], P('rep'), may hold values from -3 to 3
- w_mid: float32 [64, 64], P('rep'), may hold values from -0.75 to 0.75
- b_mid: float32 [64], P('rep'), may hold values from -3 to 3
- w_out: float32 [6, 64], P(None, 'rep'), may hold values from -0.75 to 0.75
- b_out: float32 [6], replicated, may hold values from -4 to 4
Outputs:
- final_state: float32 [2, 128, 32, 512], P(None, 'blk', 'gy', 'rep')
- loss: float32 [], replicated
- grad_w_in: float32 [64, 10], P('rep')
- grad_b_in: float32 [64], P('rep')
- grad_w_mid: float32 [64, 64], P('rep')
- grad_b_mid: float32 [64], P('rep')
- grad_w_out: float32 [6, 64], P(None, 'rep')
- grad_b_out: float32 [6], replicated
- start_sensitivity: float32 [2, 128, 32, 512], P(None, 'blk', 'gy', 'rep')
Inputs may be any that keep to these rules, and one draw needn't show every extreme that they name: `init_masks`: 0 or 1 in every cell. `target_masks`: 0 or 1 in every cell.
All inputs are finite; a program needn't handle non-finite values.
Results may differ from a plain program's by a relative error of at most 0.0054.
The roundings to bfloat16 on the way count: a program that leaves them out, or rounds other values in their place, can miss the bound.
Values may be sent and summed in bfloat16 or wider, within the bound.
A program may use at most 64 MiB of HBM per device.

v0:
```python
import jax
import jax.numpy as jnp
from jax import lax
from jax.sharding import PartitionSpec as P

STEPS = 4
RATE_MAX = 0.15
AXES = (("rep", 3), ("gy", 2), ("blk", 1))


def ring_perms(axis):
    count = lax.axis_size(axis)
    forward = [(i, (i + 1) % count) for i in range(count)]
    backward = [((i + 1) % count, i) for i in range(count)]
    return (forward, backward)


def exchange_faces(fields):
    faces = []
    for direction, (axis, dim) in enumerate(AXES):
        block = fields[direction]
        forward, backward = ring_perms(axis)
        size = block.shape[dim]
        low = lax.ppermute(lax.slice_in_dim(block, size - 1, size, axis=dim), axis, forward)
        high = lax.ppermute(lax.slice_in_dim(block, 0, 1, axis=dim), axis, backward)
        faces.append((low, high))
    return faces


def shifted(block, low, high, dim, offset):
    size = block.shape[dim]
    if offset == 1:
        return jnp.concatenate([lax.slice_in_dim(block, 1, size, axis=dim), high], axis=dim)
    return jnp.concatenate([low, lax.slice_in_dim(block, 0, size - 1, axis=dim)], axis=dim)


def diffuse(field, field_faces, rates, rate_faces):
    summed = field
    for direction, (axis, dim) in enumerate(AXES):
        rate_here = rates[direction::3]
        for offset in (1, -1):
            low, high = field_faces[direction]
            rlow, rhigh = rate_faces[direction]
            rate_next = shifted(rate_here, rlow, rhigh, dim, offset)
            summed = summed + 0.5 * (rate_here + rate_next) * (
                shifted(field, low, high, dim, offset) - field
            )
    return summed


def rate_cotangent(state, state_faces, adjoint, adjoint_faces):
    pieces_list = []
    for direction, (axis, dim) in enumerate(AXES):
        summed = jnp.zeros_like(state)
        for offset in (1, -1):
            slow, shigh = state_faces[direction]
            alow, ahigh = adjoint_faces[direction]
            summed = summed + (shifted(state, slow, shigh, dim, offset) - state) * (
                shifted(adjoint, alow, ahigh, dim, offset) - adjoint
            )
        pieces_list.append(-0.5 * summed)
    stacked = jnp.stack(pieces_list, axis=1)
    return stacked.reshape((6,) + stacked.shape[2:])


def embed_lookup(emb_table, grain_flat):
    table_rows = emb_table.shape[0]
    one_hot = (grain_flat[None, :] == lax.broadcasted_iota(jnp.int32, (table_rows, 1), 0)).astype(
        jnp.bfloat16
    )
    looked = jnp.dot(emb_table.T, one_hot, preferred_element_type=jnp.float32)
    return looked.astype(jnp.bfloat16)


def forward_layers(params, features):
    w_in, b_in, w_mid, b_mid, w_out, b_out = params
    act_one = jnp.tanh(
        jnp.dot(w_in, features, preferred_element_type=jnp.float32)
        + b_in.astype(jnp.float32)[:, None]
    )
    hid_one = act_one.astype(jnp.bfloat16)
    act_two = jnp.tanh(
        jnp.dot(w_mid, hid_one, preferred_element_type=jnp.float32)
        + b_mid.astype(jnp.float32)[:, None]
    )
    hid_two = act_two.astype(jnp.bfloat16)
    logits = (
        jnp.dot(w_out, hid_two, preferred_element_type=jnp.float32)
        + b_out.astype(jnp.float32)[:, None]
    )
    return (RATE_MAX * jax.nn.sigmoid(logits), act_one, hid_one, act_two, hid_two)


def backward_layers(params, features, rate_grad, forward_values):
    w_in, b_in, w_mid, b_mid, w_out, b_out = params
    rate_values, act_one, hid_one, act_two, hid_two = forward_values
    out_grad = (rate_grad * rate_values * (1.0 - rate_values / RATE_MAX)).astype(jnp.bfloat16)
    two_grad = (
        jnp.dot(w_out.T, out_grad, preferred_element_type=jnp.float32) * (1.0 - act_two * act_two)
    ).astype(jnp.bfloat16)
    one_grad = (
        jnp.dot(w_mid.T, two_grad, preferred_element_type=jnp.float32) * (1.0 - act_one * act_one)
    ).astype(jnp.bfloat16)
    grad_terms = (
        jnp.dot(one_grad, features.T, preferred_element_type=jnp.float32),
        jnp.sum(one_grad, axis=1, dtype=jnp.float32),
        jnp.dot(two_grad, hid_one.T, preferred_element_type=jnp.float32),
        jnp.sum(two_grad, axis=1, dtype=jnp.float32),
        jnp.dot(out_grad, hid_two.T, preferred_element_type=jnp.float32),
        jnp.sum(out_grad, axis=1, dtype=jnp.float32),
    )
    state_grad = jnp.dot(w_in[:, -2:].T, one_grad, preferred_element_type=jnp.float32)
    return (grad_terms, state_grad)


def gather_params(w_in, b_in, w_mid, b_mid, w_out, b_out):
    n_in = w_in.shape[1]
    n_mid = w_mid.shape[1]
    packed = jnp.concatenate([w_in, b_in[:, None], w_mid, b_mid[:, None], w_out.T], axis=1).astype(
        jnp.bfloat16
    )
    full = lax.all_gather(packed, "rep", axis=0, tiled=True)
    col = 0
    w_in_b = full[:, col : col + n_in]
    col += n_in
    b_in_b = full[:, col]
    col += 1
    w_mid_b = full[:, col : col + n_mid]
    col += n_mid
    b_mid_b = full[:, col]
    col += 1
    w_out_b = full[:, col:].T
    return (w_in_b, b_in_b, w_mid_b, b_mid_b, w_out_b, b_out.astype(jnp.bfloat16))


def per_device(
    grain_id, init_masks, target_masks, emb_table, w_in, b_in, w_mid, b_mid, w_out, b_out
):
    params = gather_params(w_in, b_in, w_mid, b_mid, w_out, b_out)
    depth_cells, row_cells, col_cells = grain_id.shape
    cell_count = depth_cells * row_cells * col_cells
    block_shape = (depth_cells, row_cells, col_cells)
    embedding = embed_lookup(emb_table, grain_id.reshape(cell_count))
    state_now = init_masks.astype(jnp.float32)
    history = []
    for step_index in range(STEPS):
        features = jnp.concatenate(
            [embedding, state_now.reshape(2, cell_count).astype(jnp.bfloat16)], axis=0
        )
        rate_values = forward_layers(params, features)[0].reshape((6,) + block_shape)
        faces = exchange_faces(
            [jnp.concatenate([state_now, rate_values[d::3]], axis=0) for d in range(3)]
        )
        state_faces = [(low[:2], high[:2]) for low, high in faces]
        rate_faces = [(low[2:], high[2:]) for low, high in faces]
        history.append((state_now, state_faces, rate_values, rate_faces))
        state_now = diffuse(state_now, state_faces, rate_values, rate_faces)
    misfit = state_now - target_masks.astype(jnp.float32)
    total_cells = float(
        cell_count * lax.axis_size("blk") * lax.axis_size("gy") * lax.axis_size("rep")
    )
    loss_part = jnp.sum(misfit * misfit) / (4.0 * total_cells)
    adjoint = misfit / (2.0 * total_cells)
    grad_sums = None
    for step_index in reversed(range(STEPS)):
        state_t, state_faces, rate_values, rate_faces = history[step_index]
        adjoint_faces = exchange_faces([adjoint] * 3)
        rate_grad = rate_cotangent(state_t, state_faces, adjoint, adjoint_faces).reshape(
            6, cell_count
        )
        features = jnp.concatenate(
            [embedding, state_t.reshape(2, cell_count).astype(jnp.bfloat16)], axis=0
        )
        forward_values = forward_layers(params, features)
        step_terms, state_grad = backward_layers(params, features, rate_grad, forward_values)
        if grad_sums is None:
            grad_sums = step_terms
        else:
            grad_sums = tuple(
                (earlier + later_term for earlier, later_term in zip(grad_sums, step_terms))
            )
        adjoint = diffuse(adjoint, adjoint_faces, rate_values, rate_faces) + state_grad.reshape(
            (2,) + block_shape
        )
    start_sensitivity = adjoint * (2.0 * total_cells)
    pieces = list(grad_sums) + [loss_part[None]]
    flat = jnp.concatenate([piece.reshape(-1) for piece in pieces])
    summed_flat = lax.psum(flat, ("blk", "gy", "rep"))
    summed = []
    start = 0
    for piece in pieces:
        summed.append(summed_flat[start : start + piece.size].reshape(piece.shape))
        start += piece.size
    position = lax.axis_index("rep")
    share_width = w_in.shape[0]
    grad_w_in = lax.dynamic_slice_in_dim(summed[0], position * share_width, share_width, 0)
    grad_b_in = lax.dynamic_slice_in_dim(summed[1], position * share_width, share_width, 0)
    grad_w_mid = lax.dynamic_slice_in_dim(summed[2], position * share_width, share_width, 0)
    grad_b_mid = lax.dynamic_slice_in_dim(summed[3], position * share_width, share_width, 0)
    grad_w_out = lax.dynamic_slice_in_dim(summed[4], position * share_width, share_width, 1)
    grad_b_out = summed[5]
    loss_total = summed[6][0]
    return (
        state_now,
        loss_total,
        grad_w_in,
        grad_b_in,
        grad_w_mid,
        grad_b_mid,
        grad_w_out,
        grad_b_out,
        start_sensitivity,
    )


def solution(mesh):
    in_specs = (
        P("blk", "gy", "rep"),
        P(None, "blk", "gy", "rep"),
        P(None, "blk", "gy", "rep"),
        P(),
        P("rep", None),
        P("rep"),
        P("rep", None),
        P("rep"),
        P(None, "rep"),
        P(),
    )
    out_specs = (
        P(None, "blk", "gy", "rep"),
        P(),
        P("rep", None),
        P("rep"),
        P("rep", None),
        P("rep"),
        P(None, "rep"),
        P(),
        P(None, "blk", "gy", "rep"),
    )
    return jax.shard_map(
        per_device, mesh=mesh, in_specs=in_specs, out_specs=out_specs, check_vma=False
    )
```

profile of v0, /device:TPU:1, one launch (start us, length us, event | category | flops | bytes accessed | tf_op | source)
XLA Modules:
  0.0 383.7 jit_solution(16146299786309421557)
XLA Ops:
  5.6 13.3 %all_gather.3 = bf16[64,82]{1,0:T(8,128)(2,1)S(1)} all-gather(bf16[16,82]{1,0:T(8,128)(2,1)S(1)} %concatenate.347), channel_id=1, replica_groups=mesh['blk'=32,'gy'=4,'rep'=4] {'rep'}, dimensions={0}, use_global_device_ids=true | all-gather | bytes 13120 | tf_op jit(solution)/shard_map/all_gather | solution.py:122
  30.3 7.8 %collective-permute-start.4 = (f32[4,1,8,128]{3,2,1,0:T(8,128)S(1)}, f32[4,1,8,128]{3,2,1,0:T(8,128)S(1)}, u32[]{:S(2)}, u32[]{:S(2)}) collective-permute-start(f32[4,1,8,128]{3,2,1,0:T(8,128)S(1)} %get-tuple-element.85), channel_id=1, source_target_pairs={{16,0},{32,16},{48,32},{64,48},{80,64},{96,80},{112,96},{128,112},... | collective-permute-start | bytes 49160 | tf_op jit(solution)/shard_map/ppermute | solution.py:25
  43.1 4.2 %collective-permute-done = f32[4,4,8,1]{3,2,1,0:T(8,128)S(1)} collective-permute-done((f32[4,4,8,1]{3,2,1,0:T(8,128)S(1)}, f32[4,4,8,1]{3,2,1,0:T(8,128)S(1)}, u32[]{:S(2)}, u32[]{:S(2)}) %collective-permute-start) | collective-permute-done | bytes 544 | tf_op jit(solution)/shard_map/ppermute | solution.py:25
  54.9 5.5 %collective-permute-start.6 = (f32[4,4,8,1]{3,2,1,0:T(8,128)S(1)}, f32[4,4,8,1]{3,2,1,0:T(8,128)S(1)}, u32[]{:S(2)}, u32[]{:S(2)}) collective-permute-start(f32[4,4,8,1]{3,2,1,0:T(8,128)S(1)} %get-tuple-element.69), channel_id=1, source_target_pairs={{1,0},{2,1},{3,2},{0,3},{5,4},{6,5},{7,6},{4,7},{9,8},{10,9},{11,1... | collective-permute-start | bytes 1544 | tf_op jit(solution)/shard_map/ppermute | solution.py:25
  60.4 4.6 %collective-permute-start.8 = (f32[4,4,1,128]{3,2,1,0:T(1,128)S(1)}, f32[4,4,1,128]{3,2,1,0:T(1,128)S(1)}, u32[]{:S(2)}, u32[]{:S(2)}) collective-permute-start(f32[4,4,1,128]{3,2,1,0:T(1,128)S(1)} %get-tuple-element.73), channel_id=1, source_target_pairs={{4,0},{8,4},{12,8},{0,12},{5,1},{9,5},{13,9},{1,13},{6,2},{10,6},{... | collective-permute-start | bytes 24584 | tf_op jit(solution)/shard_map/ppermute | solution.py:25
  66.9 4.9 %collective-permute-start.10 = (f32[4,1,8,128]{3,2,1,0:T(8,128)S(1)}, f32[4,1,8,128]{3,2,1,0:T(8,128)S(1)}, u32[]{:S(2)}, u32[]{:S(2)}) collective-permute-start(f32[4,1,8,128]{3,2,1,0:T(8,128)S(1)} %get-tuple-element.75), channel_id=1, source_target_pairs={{16,0},{32,16},{48,32},{64,48},{80,64},{96,80},{112,96},{128,112},... | collective-permute-start | bytes 49160 | tf_op jit(solution)/shard_map/ppermute | solution.py:25
  73.7 3.9 %collective-permute-start.7 = (f32[4,4,8,1]{3,2,1,0:T(8,128)S(1)}, f32[4,4,8,1]{3,2,1,0:T(8,128)S(1)}, u32[]{:S(2)}, u32[]{:S(2)}) collective-permute-start(f32[4,4,8,1]{3,2,1,0:T(8,128)S(1)} %get-tuple-element.70), channel_id=1, source_target_pairs={{0,1},{1,2},{2,3},{3,0},{4,5},{5,6},{6,7},{7,4},{8,9},{9,10},{10,1... | collective-permute-start | bytes 1544 | tf_op jit(solution)/shard_map/ppermute | solution.py:24
  83.5 4.3 %collective-permute-start.12 = (f32[4,4,8,1]{3,2,1,0:T(8,128)S(1)}, f32[4,4,8,1]{3,2,1,0:T(8,128)S(1)}, u32[]{:S(2)}, u32[]{:S(2)}) collective-permute-start(f32[4,4,8,1]{3,2,1,0:T(8,128)S(1)} %get-tuple-element.59), channel_id=1, source_target_pairs={{1,0},{2,1},{3,2},{0,3},{5,4},{6,5},{7,6},{4,7},{9,8},{10,9},{11,1... | collective-permute-start | bytes 1544 | tf_op jit(solution)/shard_map/ppermute | solution.py:25
  87.8 4.8 %collective-permute-start.14 = (f32[4,4,1,128]{3,2,1,0:T(1,128)S(1)}, f32[4,4,1,128]{3,2,1,0:T(1,128)S(1)}, u32[]{:S(2)}, u32[]{:S(2)}) collective-permute-start(f32[4,4,1,128]{3,2,1,0:T(1,128)S(1)} %get-tuple-element.63), channel_id=1, source_target_pairs={{4,0},{8,4},{12,8},{0,12},{5,1},{9,5},{13,9},{1,13},{6,2},{10,6},{... | collective-permute-start | bytes 24584 | tf_op jit(solution)/shard_map/ppermute | solution.py:25
  94.6 5.8 %collective-permute-start.16 = (f32[4,1,8,128]{3,2,1,0:T(8,128)S(1)}, f32[4,1,8,128]{3,2,1,0:T(8,128)S(1)}, u32[]{:S(2)}, u32[]{:S(2)}) collective-permute-start(f32[4,1,8,128]{3,2,1,0:T(8,128)S(1)} %get-tuple-element.65), channel_id=1, source_target_pairs={{16,0},{32,16},{48,32},{64,48},{80,64},{96,80},{112,96},{128,112},... | collective-permute-start | bytes 49160 | tf_op jit(solution)/shard_map/ppermute | solution.py:25
  102.3 3.9 %collective-permute-start.13 = (f32[4,4,8,1]{3,2,1,0:T(8,128)S(1)}, f32[4,4,8,1]{3,2,1,0:T(8,128)S(1)}, u32[]{:S(2)}, u32[]{:S(2)}) collective-permute-start(f32[4,4,8,1]{3,2,1,0:T(8,128)S(1)} %get-tuple-element.60), channel_id=1, source_target_pairs={{0,1},{1,2},{2,3},{3,0},{4,5},{5,6},{6,7},{7,4},{8,9},{9,10},{10,1... | collective-permute-start | bytes 1544 | tf_op jit(solution)/shard_map/ppermute | solution.py:24
  111.7 4.3 %collective-permute-start.18 = (f32[4,4,8,1]{3,2,1,0:T(8,128)S(1)}, f32[4,4,8,1]{3,2,1,0:T(8,128)S(1)}, u32[]{:S(2)}, u32[]{:S(2)}) collective-permute-start(f32[4,4,8,1]{3,2,1,0:T(8,128)S(1)} %get-tuple-element.49), channel_id=1, source_target_pairs={{1,0},{2,1},{3,2},{0,3},{5,4},{6,5},{7,6},{4,7},{9,8},{10,9},{11,1... | collective-permute-start | bytes 1544 | tf_op jit(solution)/shard_map/ppermute | solution.py:25
  116.0 4.9 %collective-permute-start.20 = (f32[4,4,1,128]{3,2,1,0:T(1,128)S(1)}, f32[4,4,1,128]{3,2,1,0:T(1,128)S(1)}, u32[]{:S(2)}, u32[]{:S(2)}) collective-permute-start(f32[4,4,1,128]{3,2,1,0:T(1,128)S(1)} %get-tuple-element.53), channel_id=1, source_target_pairs={{4,0},{8,4},{12,8},{0,12},{5,1},{9,5},{13,9},{1,13},{6,2},{10,6},{... | collective-permute-start | bytes 24584 | tf_op jit(solution)/shard_map/ppermute | solution.py:25
  122.8 5.8 %collective-permute-start.22 = (f32[4,1,8,128]{3,2,1,0:T(8,128)S(1)}, f32[4,1,8,128]{3,2,1,0:T(8,128)S(1)}, u32[]{:S(2)}, u32[]{:S(2)}) collective-permute-start(f32[4,1,8,128]{3,2,1,0:T(8,128)S(1)} %get-tuple-element.55), channel_id=1, source_target_pairs={{16,0},{32,16},{48,32},{64,48},{80,64},{96,80},{112,96},{128,112},... | collective-permute-start | bytes 49160 | tf_op jit(solution)/shard_map/ppermute | solution.py:25
  140.1 4.8 %collective-permute-start.26 = (f32[2,4,1,128]{3,2,1,0:T(1,128)}, f32[2,4,1,128]{3,2,1,0:T(1,128)}, u32[]{:S(2)}, u32[]{:S(2)}) collective-permute-start(f32[2,4,1,128]{3,2,1,0:T(1,128)} %get-tuple-element.129), channel_id=1, source_target_pairs={{4,0},{8,4},{12,8},{0,12},{5,1},{9,5},{13,9},{1,13},{6,2},{10,6},{... | collective-permute-start | bytes 12296 | tf_op jit(solution)/shard_map/ppermute | solution.py:25
  147.5 5.1 %collective-permute-start.28 = (f32[2,1,8,128]{3,2,1,0:T(8,128)}, f32[2,1,8,128]{3,2,1,0:T(8,128)}, u32[]{:S(2)}, u32[]{:S(2)}) collective-permute-start(f32[2,1,8,128]{3,2,1,0:T(8,128)} %get-tuple-element.133), channel_id=1, source_target_pairs={{16,0},{32,16},{48,32},{64,48},{80,64},{96,80},{112,96},{128,112},... | collective-permute-start | bytes 24584 | tf_op jit(solution)/shard_map/ppermute | solution.py:25
  152.6 5.5 %collective-permute-start.24 = (f32[2,4,8,1]{3,2,1,0:T(8,128)}, f32[2,4,8,1]{3,2,1,0:T(8,128)}, u32[]{:S(2)}, u32[]{:S(2)}) collective-permute-start(f32[2,4,8,1]{3,2,1,0:T(8,128)} %get-tuple-element.125), channel_id=1, source_target_pairs={{1,0},{2,1},{3,2},{0,3},{5,4},{6,5},{7,6},{4,7},{9,8},{10,9},{11,1... | collective-permute-start | bytes 776 | tf_op jit(solution)/shard_map/ppermute | solution.py:25
  181.7 4.8 %collective-permute-start.32 = (f32[2,4,1,128]{3,2,1,0:T(1,128)S(1)}, f32[2,4,1,128]{3,2,1,0:T(1,128)S(1)}, u32[]{:S(2)}, u32[]{:S(2)}) collective-permute-start(f32[2,4,1,128]{3,2,1,0:T(1,128)S(1)} %get-tuple-element.117), channel_id=1, source_target_pairs={{4,0},{8,4},{12,8},{0,12},{5,1},{9,5},{13,9},{1,13},{6,2},{10,6},{... | collective-permute-start | bytes 12296 | tf_op jit(solution)/shard_map/ppermute | solution.py:25
  190.9 4.7 %collective-permute-start.31 = (f32[2,4,8,1]{3,2,1,0:T(8,128)S(1)}, f32[2,4,8,1]{3,2,1,0:T(8,128)S(1)}, u32[]{:S(2)}, u32[]{:S(2)}) collective-permute-start(f32[2,4,8,1]{3,2,1,0:T(8,128)S(1)} %get-tuple-element.114), channel_id=1, source_target_pairs={{0,1},{1,2},{2,3},{3,0},{4,5},{5,6},{6,7},{7,4},{8,9},{9,10},{10,1... | collective-permute-start | bytes 776 | tf_op jit(solution)/shard_map/ppermute | solution.py:24
  216.0 4.6 %collective-permute-start.38 = (f32[2,4,1,128]{3,2,1,0:T(1,128)S(1)}, f32[2,4,1,128]{3,2,1,0:T(1,128)S(1)}, u32[]{:S(2)}, u32[]{:S(2)}) collective-permute-start(f32[2,4,1,128]{3,2,1,0:T(1,128)S(1)} %get-tuple-element.105), channel_id=1, source_target_pairs={{4,0},{8,4},{12,8},{0,12},{5,1},{9,5},{13,9},{1,13},{6,2},{10,6},{... | collective-permute-start | bytes 12296 | tf_op jit(solution)/shard_map/ppermute | solution.py:25
  224.4 5.1 %collective-permute-start.37 = (f32[2,4,8,1]{3,2,1,0:T(8,128)S(1)}, f32[2,4,8,1]{3,2,1,0:T(8,128)S(1)}, u32[]{:S(2)}, u32[]{:S(2)}) collective-permute-start(f32[2,4,8,1]{3,2,1,0:T(8,128)S(1)} %get-tuple-element.102), channel_id=1, source_target_pairs={{0,1},{1,2},{2,3},{3,0},{4,5},{5,6},{6,7},{7,4},{8,9},{9,10},{10,1... | collective-permute-start | bytes 776 | tf_op jit(solution)/shard_map/ppermute | solution.py:24
  249.8 4.6 %collective-permute-start.44 = (f32[2,4,1,128]{3,2,1,0:T(1,128)S(1)}, f32[2,4,1,128]{3,2,1,0:T(1,128)S(1)}, u32[]{:S(2)}, u32[]{:S(2)}) collective-permute-start(f32[2,4,1,128]{3,2,1,0:T(1,128)S(1)} %get-tuple-element.93), channel_id=1, source_target_pairs={{4,0},{8,4},{12,8},{0,12},{5,1},{9,5},{13,9},{1,13},{6,2},{10,6},{... | collective-permute-start | bytes 12296 | tf_op jit(solution)/shard_map/ppermute | solution.py:25
  258.5 4.8 %collective-permute-start.43 = (f32[2,4,8,1]{3,2,1,0:T(8,128)S(1)}, f32[2,4,8,1]{3,2,1,0:T(8,128)S(1)}, u32[]{:S(2)}, u32[]{:S(2)}) collective-permute-start(f32[2,4,8,1]{3,2,1,0:T(8,128)S(1)} %get-tuple-element.90), channel_id=1, source_target_pairs={{0,1},{1,2},{2,3},{3,0},{4,5},{5,6},{6,7},{7,4},{8,9},{9,10},{10,1... | collective-permute-start | bytes 776 | tf_op jit(solution)/shard_map/ppermute | solution.py:24
  276.9 101.3 %psum.7 = f32[5255]{0:T(1024)S(1)} all-reduce(f32[5255]{0:T(1024)S(1)} %concatenate.436), channel_id=1, replica_groups=mesh['blk'=32,'gy'=4,'rep'=4] {'blk','gy','rep'}, use_global_device_ids=true, to_apply=%region_13.0 | all-reduce | flops 5255 | bytes 42040 | tf_op jit(solution)/shard_map/psum | solution.py:188
  (875 shorter events, 153.9 us)
Async XLA Ops:
  25.0 25.5 %collective-permute-start.2 = (f32[4,4,1,128]{3,2,1,0:T(1,128)S(1)}, f32[4,4,1,128]{3,2,1,0:T(1,128)S(1)}, u32[]{:S(2)}, u32[]{:S(2)}) collective-permute-start(f32[4,4,1,128]{3,2,1,0:T(1,128)S(1)} %get-tuple-element.83), channel_id=1, source_target_pairs={{4,0},{8,4},{12,8},{0,12},{5,1},{9,5},{13,9},{1,13},{6,2},{10,6},{... | collective-permute-start | bytes 24584 | tf_op jit(solution)/shard_map/ppermute | solution.py:25
  26.9 23.6 %collective-permute-start.3 = (f32[4,4,1,128]{3,2,1,0:T(1,128)S(1)}, f32[4,4,1,128]{3,2,1,0:T(1,128)S(1)}, u32[]{:S(2)}, u32[]{:S(2)}) collective-permute-start(f32[4,4,1,128]{3,2,1,0:T(1,128)S(1)} %get-tuple-element.84), channel_id=1, source_target_pairs={{0,4},{4,8},{8,12},{12,0},{1,5},{5,9},{9,13},{13,1},{2,6},{6,10},{... | collective-permute-start | bytes 24584 | tf_op jit(solution)/shard_map/ppermute | solution.py:24
  30.3 20.2 %collective-permute-start.4 = (f32[4,1,8,128]{3,2,1,0:T(8,128)S(1)}, f32[4,1,8,128]{3,2,1,0:T(8,128)S(1)}, u32[]{:S(2)}, u32[]{:S(2)}) collective-permute-start(f32[4,1,8,128]{3,2,1,0:T(8,128)S(1)} %get-tuple-element.85), channel_id=1, source_target_pairs={{16,0},{32,16},{48,32},{64,48},{80,64},{96,80},{112,96},{128,112},... | collective-permute-start | bytes 49160 | tf_op jit(solution)/shard_map/ppermute | solution.py:25
  38.1 12.5 %collective-permute-start.5 = (f32[4,1,8,128]{3,2,1,0:T(8,128)S(1)}, f32[4,1,8,128]{3,2,1,0:T(8,128)S(1)}, u32[]{:S(2)}, u32[]{:S(2)}) collective-permute-start(f32[4,1,8,128]{3,2,1,0:T(8,128)S(1)} %get-tuple-element.86), channel_id=1, source_target_pairs={{0,16},{16,32},{32,48},{48,64},{64,80},{80,96},{96,112},{112,128},... | collective-permute-start | bytes 49160 | tf_op jit(solution)/shard_map/ppermute | solution.py:24
  54.9 18.8 %collective-permute-start.6 = (f32[4,4,8,1]{3,2,1,0:T(8,128)S(1)}, f32[4,4,8,1]{3,2,1,0:T(8,128)S(1)}, u32[]{:S(2)}, u32[]{:S(2)}) collective-permute-start(f32[4,4,8,1]{3,2,1,0:T(8,128)S(1)} %get-tuple-element.69), channel_id=1, source_target_pairs={{1,0},{2,1},{3,2},{0,3},{5,4},{6,5},{7,6},{4,7},{9,8},{10,9},{11,1... | collective-permute-start | bytes 1544 | tf_op jit(solution)/shard_map/ppermute | solution.py:25
  60.4 18.6 %collective-permute-start.8 = (f32[4,4,1,128]{3,2,1,0:T(1,128)S(1)}, f32[4,4,1,128]{3,2,1,0:T(1,128)S(1)}, u32[]{:S(2)}, u32[]{:S(2)}) collective-permute-start(f32[4,4,1,128]{3,2,1,0:T(1,128)S(1)} %get-tuple-element.73), channel_id=1, source_target_pairs={{4,0},{8,4},{12,8},{0,12},{5,1},{9,5},{13,9},{1,13},{6,2},{10,6},{... | collective-permute-start | bytes 24584 | tf_op jit(solution)/shard_map/ppermute | solution.py:25
  65.0 14.1 %collective-permute-start.9 = (f32[4,4,1,128]{3,2,1,0:T(1,128)S(1)}, f32[4,4,1,128]{3,2,1,0:T(1,128)S(1)}, u32[]{:S(2)}, u32[]{:S(2)}) collective-permute-start(f32[4,4,1,128]{3,2,1,0:T(1,128)S(1)} %get-tuple-element.74), channel_id=1, source_target_pairs={{0,4},{4,8},{8,12},{12,0},{1,5},{5,9},{9,13},{13,1},{2,6},{6,10},{... | collective-permute-start | bytes 24584 | tf_op jit(solution)/shard_map/ppermute | solution.py:24
  83.5 18.8 %collective-permute-start.12 = (f32[4,4,8,1]{3,2,1,0:T(8,128)S(1)}, f32[4,4,8,1]{3,2,1,0:T(8,128)S(1)}, u32[]{:S(2)}, u32[]{:S(2)}) collective-permute-start(f32[4,4,8,1]{3,2,1,0:T(8,128)S(1)} %get-tuple-element.59), channel_id=1, source_target_pairs={{1,0},{2,1},{3,2},{0,3},{5,4},{6,5},{7,6},{4,7},{9,8},{10,9},{11,1... | collective-permute-start | bytes 1544 | tf_op jit(solution)/shard_map/ppermute | solution.py:25
  87.8 19.8 %collective-permute-start.14 = (f32[4,4,1,128]{3,2,1,0:T(1,128)S(1)}, f32[4,4,1,128]{3,2,1,0:T(1,128)S(1)}, u32[]{:S(2)}, u32[]{:S(2)}) collective-permute-start(f32[4,4,1,128]{3,2,1,0:T(1,128)S(1)} %get-tuple-element.63), channel_id=1, source_target_pairs={{4,0},{8,4},{12,8},{0,12},{5,1},{9,5},{13,9},{1,13},{6,2},{10,6},{... | collective-permute-start | bytes 24584 | tf_op jit(solution)/shard_map/ppermute | solution.py:25
  92.6 15.0 %collective-permute-start.15 = (f32[4,4,1,128]{3,2,1,0:T(1,128)S(1)}, f32[4,4,1,128]{3,2,1,0:T(1,128)S(1)}, u32[]{:S(2)}, u32[]{:S(2)}) collective-permute-start(f32[4,4,1,128]{3,2,1,0:T(1,128)S(1)} %get-tuple-element.64), channel_id=1, source_target_pairs={{0,4},{4,8},{8,12},{12,0},{1,5},{5,9},{9,13},{13,1},{2,6},{6,10},{... | collective-permute-start | bytes 24584 | tf_op jit(solution)/shard_map/ppermute | solution.py:24
  94.6 13.1 %collective-permute-start.16 = (f32[4,1,8,128]{3,2,1,0:T(8,128)S(1)}, f32[4,1,8,128]{3,2,1,0:T(8,128)S(1)}, u32[]{:S(2)}, u32[]{:S(2)}) collective-permute-start(f32[4,1,8,128]{3,2,1,0:T(8,128)S(1)} %get-tuple-element.65), channel_id=1, source_target_pairs={{16,0},{32,16},{48,32},{64,48},{80,64},{96,80},{112,96},{128,112},... | collective-permute-start | bytes 49160 | tf_op jit(solution)/shard_map/ppermute | solution.py:25
  111.7 18.8 %collective-permute-start.18 = (f32[4,4,8,1]{3,2,1,0:T(8,128)S(1)}, f32[4,4,8,1]{3,2,1,0:T(8,128)S(1)}, u32[]{:S(2)}, u32[]{:S(2)}) collective-permute-start(f32[4,4,8,1]{3,2,1,0:T(8,128)S(1)} %get-tuple-element.49), channel_id=1, source_target_pairs={{1,0},{2,1},{3,2},{0,3},{5,4},{6,5},{7,6},{4,7},{9,8},{10,9},{11,1... | collective-permute-start | bytes 1544 | tf_op jit(solution)/shard_map/ppermute | solution.py:25
  116.0 19.8 %collective-permute-start.20 = (f32[4,4,1,128]{3,2,1,0:T(1,128)S(1)}, f32[4,4,1,128]{3,2,1,0:T(1,128)S(1)}, u32[]{:S(2)}, u32[]{:S(2)}) collective-permute-start(f32[4,4,1,128]{3,2,1,0:T(1,128)S(1)} %get-tuple-element.53), channel_id=1, source_target_pairs={{4,0},{8,4},{12,8},{0,12},{5,1},{9,5},{13,9},{1,13},{6,2},{10,6},{... | collective-permute-start | bytes 24584 | tf_op jit(solution)/shard_map/ppermute | solution.py:25
  120.9 15.0 %collective-permute-start.21 = (f32[4,4,1,128]{3,2,1,0:T(1,128)S(1)}, f32[4,4,1,128]{3,2,1,0:T(1,128)S(1)}, u32[]{:S(2)}, u32[]{:S(2)}) collective-permute-start(f32[4,4,1,128]{3,2,1,0:T(1,128)S(1)} %get-tuple-element.54), channel_id=1, source_target_pairs={{0,4},{4,8},{8,12},{12,0},{1,5},{5,9},{9,13},{13,1},{2,6},{6,10},{... | collective-permute-start | bytes 24584 | tf_op jit(solution)/shard_map/ppermute | solution.py:24
  122.8 13.1 %collective-permute-start.22 = (f32[4,1,8,128]{3,2,1,0:T(8,128)S(1)}, f32[4,1,8,128]{3,2,1,0:T(8,128)S(1)}, u32[]{:S(2)}, u32[]{:S(2)}) collective-permute-start(f32[4,1,8,128]{3,2,1,0:T(8,128)S(1)} %get-tuple-element.55), channel_id=1, source_target_pairs={{16,0},{32,16},{48,32},{64,48},{80,64},{96,80},{112,96},{128,112},... | collective-permute-start | bytes 49160 | tf_op jit(solution)/shard_map/ppermute | solution.py:25
  140.1 24.1 %collective-permute-start.26 = (f32[2,4,1,128]{3,2,1,0:T(1,128)}, f32[2,4,1,128]{3,2,1,0:T(1,128)}, u32[]{:S(2)}, u32[]{:S(2)}) collective-permute-start(f32[2,4,1,128]{3,2,1,0:T(1,128)} %get-tuple-element.129), channel_id=1, source_target_pairs={{4,0},{8,4},{12,8},{0,12},{5,1},{9,5},{13,9},{1,13},{6,2},{10,6},{... | collective-permute-start | bytes 12296 | tf_op jit(solution)/shard_map/ppermute | solution.py:25
  144.9 19.2 %collective-permute-start.27 = (f32[2,4,1,128]{3,2,1,0:T(1,128)}, f32[2,4,1,128]{3,2,1,0:T(1,128)}, u32[]{:S(2)}, u32[]{:S(2)}) collective-permute-start(f32[2,4,1,128]{3,2,1,0:T(1,128)} %get-tuple-element.130), channel_id=1, source_target_pairs={{0,4},{4,8},{8,12},{12,0},{1,5},{5,9},{9,13},{13,1},{2,6},{6,10},{... | collective-permute-start | bytes 12296 | tf_op jit(solution)/shard_map/ppermute | solution.py:24
  147.5 17.7 %collective-permute-start.28 = (f32[2,1,8,128]{3,2,1,0:T(8,128)}, f32[2,1,8,128]{3,2,1,0:T(8,128)}, u32[]{:S(2)}, u32[]{:S(2)}) collective-permute-start(f32[2,1,8,128]{3,2,1,0:T(8,128)} %get-tuple-element.133), channel_id=1, source_target_pairs={{16,0},{32,16},{48,32},{64,48},{80,64},{96,80},{112,96},{128,112},... | collective-permute-start | bytes 24584 | tf_op jit(solution)/shard_map/ppermute | solution.py:25
  181.7 19.4 %collective-permute-start.32 = (f32[2,4,1,128]{3,2,1,0:T(1,128)S(1)}, f32[2,4,1,128]{3,2,1,0:T(1,128)S(1)}, u32[]{:S(2)}, u32[]{:S(2)}) collective-permute-start(f32[2,4,1,128]{3,2,1,0:T(1,128)S(1)} %get-tuple-element.117), channel_id=1, source_target_pairs={{4,0},{8,4},{12,8},{0,12},{5,1},{9,5},{13,9},{1,13},{6,2},{10,6},{... | collective-permute-start | bytes 12296 | tf_op jit(solution)/shard_map/ppermute | solution.py:25
  186.6 14.6 %collective-permute-start.33 = (f32[2,4,1,128]{3,2,1,0:T(1,128)S(1)}, f32[2,4,1,128]{3,2,1,0:T(1,128)S(1)}, u32[]{:S(2)}, u32[]{:S(2)}) collective-permute-start(f32[2,4,1,128]{3,2,1,0:T(1,128)S(1)} %get-tuple-element.118), channel_id=1, source_target_pairs={{0,4},{4,8},{8,12},{12,0},{1,5},{5,9},{9,13},{13,1},{2,6},{6,10},{... | collective-permute-start | bytes 12296 | tf_op jit(solution)/shard_map/ppermute | solution.py:24
  216.0 18.9 %collective-permute-start.38 = (f32[2,4,1,128]{3,2,1,0:T(1,128)S(1)}, f32[2,4,1,128]{3,2,1,0:T(1,128)S(1)}, u32[]{:S(2)}, u32[]{:S(2)}) collective-permute-start(f32[2,4,1,128]{3,2,1,0:T(1,128)S(1)} %get-tuple-element.105), channel_id=1, source_target_pairs={{4,0},{8,4},{12,8},{0,12},{5,1},{9,5},{13,9},{1,13},{6,2},{10,6},{... | collective-permute-start | bytes 12296 | tf_op jit(solution)/shard_map/ppermute | solution.py:25
  220.5 14.4 %collective-permute-start.39 = (f32[2,4,1,128]{3,2,1,0:T(1,128)S(1)}, f32[2,4,1,128]{3,2,1,0:T(1,128)S(1)}, u32[]{:S(2)}, u32[]{:S(2)}) collective-permute-start(f32[2,4,1,128]{3,2,1,0:T(1,128)S(1)} %get-tuple-element.106), channel_id=1, source_target_pairs={{0,4},{4,8},{8,12},{12,0},{1,5},{5,9},{9,13},{13,1},{2,6},{6,10},{... | collective-permute-start | bytes 12296 | tf_op jit(solution)/shard_map/ppermute | solution.py:24
  249.8 18.9 %collective-permute-start.44 = (f32[2,4,1,128]{3,2,1,0:T(1,128)S(1)}, f32[2,4,1,128]{3,2,1,0:T(1,128)S(1)}, u32[]{:S(2)}, u32[]{:S(2)}) collective-permute-start(f32[2,4,1,128]{3,2,1,0:T(1,128)S(1)} %get-tuple-element.93), channel_id=1, source_target_pairs={{4,0},{8,4},{12,8},{0,12},{5,1},{9,5},{13,9},{1,13},{6,2},{10,6},{... | collective-permute-start | bytes 12296 | tf_op jit(solution)/shard_map/ppermute | solution.py:25
  254.3 14.4 %collective-permute-start.45 = (f32[2,4,1,128]{3,2,1,0:T(1,128)S(1)}, f32[2,4,1,128]{3,2,1,0:T(1,128)S(1)}, u32[]{:S(2)}, u32[]{:S(2)}) collective-permute-start(f32[2,4,1,128]{3,2,1,0:T(1,128)S(1)} %get-tuple-element.94), channel_id=1, source_target_pairs={{0,4},{4,8},{8,12},{12,0},{1,5},{5,9},{9,13},{13,1},{2,6},{6,10},{... | collective-permute-start | bytes 12296 | tf_op jit(solution)/shard_map/ppermute | solution.py:24
  (324 other events, 5158.2 us)
where the time goes:
time: 386 us; the launch traced here: 384 us
  starting transfers between devices  167 us (43%)
  blocking collectives  115 us (30%)
  matrix products  34.2 us (9%)
  local copies, waits for them, and re-layouts  22.1 us (6%)
  waiting for transfers between devices  21.5 us (6%)
  other arithmetic  17.5 us (5%)
  between operations  6.61 us (2%)
    psum x1, blocking collectives, per_device(): summed_flat = lax.psum(flat, ('blk', 'gy', 'rep'))  101 us
    ppermute x24, starting transfers between devices, exchange_faces(): high = lax.ppermute(lax.slice_in_dim(block, 0, 1, axis=dim), axis, backward)  98.7 us
    ppermute x24, starting transfers between devices, exchange_faces(): lax.ppermute(lax.slice_in_dim(block, size - 1, size, axis=dim), axis, for...  68.5 us
    ppermute x24, waiting for transfers between devices, exchange_faces(): lax.ppermute(lax.slice_in_dim(block, size - 1, size, axis=dim), axis, for...  17.3 us
    all_gather x1, blocking collectives, gather_params(): full = lax.all_gather(packed, 'rep', axis=0, tiled=True)  13.3 us
  transfers between devices with their start and end apart: 48, of which 9 were waited for; matrix products, arithmetic and copies ran while one was open for 1% of the time, Pallas kernels for 0%

commit v1 on v0

--- a/solution.py
+++ b/solution.py
@@ -185,7 +185,7 @@
     start_sensitivity = adjoint * (2.0 * total_cells)
     pieces = list(grad_sums) + [loss_part[None]]
     flat = jnp.concatenate([piece.reshape(-1) for piece in pieces])
-    summed_flat = lax.psum(flat, ("blk", "gy", "rep"))
+    summed_flat = jnp.sum(lax.all_gather(flat, ("blk", "gy", "rep")), axis=0)
     summed = []
     start = 0
     for piece in pieces:

time: 386 us -> 842 us (2.18)
  waiting for transfers between devices: 21.5 us -> 519 us
  blocking collectives: 115 us -> 13.3 us
  local copies, waits for them, and re-layouts: 22.1 us -> 45.2 us
  other arithmetic: 17.5 us -> 30.9 us
  between operations: 6.61 us -> 18.5 us
    unnamed x0 -> x2, waiting for transfers between devices: none -> 499 us
    psum x1 -> x0, blocking collectives: 101 us -> none  [per_device(): summed_flat = lax.psum(flat, ('blk', 'gy', 'rep'))]
    all_gather x0 -> x1, local copies, waits for them, and re-layouts: none -> 16 us  [per_device(): summed_flat = jnp.sum(lax.all_gather(flat, ('blk', 'gy', 'rep')), axis=0)]
    unnamed x608 -> x366, local copies, waits for them, and re-layouts: 4.83 us -> 13.5 us
  transfers between devices with their start and end apart: 48 -> 49, of which waited for: 9 -> 10; matrix products, arithmetic and copies ran while one was open for 1% -> 1% of each run, Pallas kernels for 0% -> 0%
where the time goes in v1:
time: 842 us; the launch traced here: 836 us
  waiting for transfers between devices  519 us (62%)
  starting transfers between devices  167 us (20%)
  local copies, waits for them, and re-layouts  45.2 us (5%)
  matrix products  42.1 us (5%)
  other arithmetic  30.9 us (4%)
  between operations  18.5 us (2%)
  blocking collectives  13.3 us (2%)
    unnamed x2, waiting for transfers between devices  499 us
    ppermute x24, starting transfers between devices, exchange_faces(): high = lax.ppermute(lax.slice_in_dim(block, 0, 1, axis=dim), axis, backward)  99 us
    ppermute x24, starting transfers between devices, exchange_faces(): lax.ppermute(lax.slice_in_dim(block, size - 1, size, axis=dim), axis, for...  68.2 us
  transfers between devices with their start and end apart: 49, of which 10 were waited for; matrix products, arithmetic and copies ran while one was open for 1% of the time, Pallas kernels for 0%

profile of v1, /device:TPU:1, one launch (start us, length us, event | category | flops | bytes accessed | tf_op | source)
XLA Modules:
  0.0 836.2 jit_solution(12125167427812487074)
XLA Ops:
  11.7 13.3 %all_gather.9 = bf16[64,82]{1,0:T(8,128)(2,1)S(1)} all-gather(bf16[16,82]{1,0:T(8,128)(2,1)S(1)} %concatenate.347), channel_id=1, replica_groups=mesh['blk'=32,'gy'=4,'rep'=4] {'rep'}, dimensions={0}, use_global_device_ids=true | all-gather | bytes 13120 | tf_op jit(solution)/shard_map/all_gather | solution.py:122
  33.9 7.8 collective-permute-start.4
  57.8 5.5 collective-permute-start.6
  63.4 4.6 collective-permute-start.8
  69.9 4.9 collective-permute-start.10
  88.8 4.3 collective-permute-start.12
  93.1 4.8 collective-permute-start.14
  99.9 5.8 collective-permute-start.16
  118.6 4.3 collective-permute-start.18
  122.9 4.9 collective-permute-start.20
  129.7 5.8 collective-permute-start.22
  146.9 4.8 collective-permute-start.26
  154.3 5.1 collective-permute-start.28
  159.4 5.5 collective-permute-start.24
  192.5 4.9 collective-permute-start.32
  201.8 4.6 collective-permute-start.31
  230.2 4.6 collective-permute-start.38
  238.7 5.1 collective-permute-start.37
  267.7 4.6 collective-permute-start.44
  276.2 5.1 collective-permute-start.43
  297.6 4.3 broadcast.37
  304.7 499.4 %all-reduce.3.cloned.1.call-done = f32[2690560]{0:T(1024)} async-done(((f32[2690560]{0:T(1024)}), f32[2690560]{0:T(1024)}) %all-reduce.3.cloned.1.call-update) | async-done | bytes 10762256
  804.1 16.0 %reshape.90 = f32[512,5255]{1,0:T(8,128)} reshape(f32[2690560]{0:T(1024)} %all-reduce.3.cloned.1.call-done) | data formatting | bytes 21524480 | tf_op jit(solution)/shard_map/all_gather | solution.py:188
  820.2 4.7 reduce_sum.139
  (637 shorter events, 183.1 us)
Async XLA Ops:
  7.2 796.9 %all-reduce.3.cloned.1.call-start = ((), (), s32[]{:S(2)}) async-start(), calls=%async_computation | async-start | bytes 21528576
  28.6 25.5 %collective-permute-start.2 = (f32[4,4,1,128]{3,2,1,0:T(1,128)S(1)}, f32[4,4,1,128]{3,2,1,0:T(1,128)S(1)}, u32[]{:S(2)}, u32[]{:S(2)}) collective-permute-start(f32[4,4,1,128]{3,2,1,0:T(1,128)S(1)} %get-tuple-element.83), channel_id=1, source_target_pairs={{4,0},{8,4},{12,8},{0,12},{5,1},{9,5},{13,9},{1,13},{6,2},{10,6},{... | collective-permute-start | bytes 24584 | tf_op jit(solution)/shard_map/ppermute | solution.py:25
  30.5 23.6 %collective-permute-start.3 = (f32[4,4,1,128]{3,2,1,0:T(1,128)S(1)}, f32[4,4,1,128]{3,2,1,0:T(1,128)S(1)}, u32[]{:S(2)}, u32[]{:S(2)}) collective-permute-start(f32[4,4,1,128]{3,2,1,0:T(1,128)S(1)} %get-tuple-element.84), channel_id=1, source_target_pairs={{0,4},{4,8},{8,12},{12,0},{1,5},{5,9},{9,13},{13,1},{2,6},{6,10},{... | collective-permute-start | bytes 24584 | tf_op jit(solution)/shard_map/ppermute | solution.py:24
  33.9 20.2 %collective-permute-start.4 = (f32[4,1,8,128]{3,2,1,0:T(8,128)S(1)}, f32[4,1,8,128]{3,2,1,0:T(8,128)S(1)}, u32[]{:S(2)}, u32[]{:S(2)}) collective-permute-start(f32[4,1,8,128]{3,2,1,0:T(8,128)S(1)} %get-tuple-element.85), channel_id=1, source_target_pairs={{16,0},{32,16},{48,32},{64,48},{80,64},{96,80},{112,96},{128,112},... | collective-permute-start | bytes 49160 | tf_op jit(solution)/shard_map/ppermute | solution.py:25
  57.8 18.9 %collective-permute-start.6 = (f32[4,4,8,1]{3,2,1,0:T(8,128)S(1)}, f32[4,4,8,1]{3,2,1,0:T(8,128)S(1)}, u32[]{:S(2)}, u32[]{:S(2)}) collective-permute-start(f32[4,4,8,1]{3,2,1,0:T(8,128)S(1)} %get-tuple-element.69), channel_id=1, source_target_pairs={{1,0},{2,1},{3,2},{0,3},{5,4},{6,5},{7,6},{4,7},{9,8},{10,9},{11,1... | collective-permute-start | bytes 1544 | tf_op jit(solution)/shard_map/ppermute | solution.py:25
  63.4 18.6 %collective-permute-start.8 = (f32[4,4,1,128]{3,2,1,0:T(1,128)S(1)}, f32[4,4,1,128]{3,2,1,0:T(1,128)S(1)}, u32[]{:S(2)}, u32[]{:S(2)}) collective-permute-start(f32[4,4,1,128]{3,2,1,0:T(1,128)S(1)} %get-tuple-element.73), channel_id=1, source_target_pairs={{4,0},{8,4},{12,8},{0,12},{5,1},{9,5},{13,9},{1,13},{6,2},{10,6},{... | collective-permute-start | bytes 24584 | tf_op jit(solution)/shard_map/ppermute | solution.py:25
  68.0 14.1 %collective-permute-start.9 = (f32[4,4,1,128]{3,2,1,0:T(1,128)S(1)}, f32[4,4,1,128]{3,2,1,0:T(1,128)S(1)}, u32[]{:S(2)}, u32[]{:S(2)}) collective-permute-start(f32[4,4,1,128]{3,2,1,0:T(1,128)S(1)} %get-tuple-element.74), channel_id=1, source_target_pairs={{0,4},{4,8},{8,12},{12,0},{1,5},{5,9},{9,13},{13,1},{2,6},{6,10},{... | collective-permute-start | bytes 24584 | tf_op jit(solution)/shard_map/ppermute | solution.py:24
  88.8 18.8 %collective-permute-start.12 = (f32[4,4,8,1]{3,2,1,0:T(8,128)S(1)}, f32[4,4,8,1]{3,2,1,0:T(8,128)S(1)}, u32[]{:S(2)}, u32[]{:S(2)}) collective-permute-start(f32[4,4,8,1]{3,2,1,0:T(8,128)S(1)} %get-tuple-element.59), channel_id=1, source_target_pairs={{1,0},{2,1},{3,2},{0,3},{5,4},{6,5},{7,6},{4,7},{9,8},{10,9},{11,1... | collective-permute-start | bytes 1544 | tf_op jit(solution)/shard_map/ppermute | solution.py:25
  93.1 19.8 %collective-permute-start.14 = (f32[4,4,1,128]{3,2,1,0:T(1,128)S(1)}, f32[4,4,1,128]{3,2,1,0:T(1,128)S(1)}, u32[]{:S(2)}, u32[]{:S(2)}) collective-permute-start(f32[4,4,1,128]{3,2,1,0:T(1,128)S(1)} %get-tuple-element.63), channel_id=1, source_target_pairs={{4,0},{8,4},{12,8},{0,12},{5,1},{9,5},{13,9},{1,13},{6,2},{10,6},{... | collective-permute-start | bytes 24584 | tf_op jit(solution)/shard_map/ppermute | solution.py:25
  98.0 15.0 %collective-permute-start.15 = (f32[4,4,1,128]{3,2,1,0:T(1,128)S(1)}, f32[4,4,1,128]{3,2,1,0:T(1,128)S(1)}, u32[]{:S(2)}, u32[]{:S(2)}) collective-permute-start(f32[4,4,1,128]{3,2,1,0:T(1,128)S(1)} %get-tuple-element.64), channel_id=1, source_target_pairs={{0,4},{4,8},{8,12},{12,0},{1,5},{5,9},{9,13},{13,1},{2,6},{6,10},{... | collective-permute-start | bytes 24584 | tf_op jit(solution)/shard_map/ppermute | solution.py:24
  99.9 13.1 %collective-permute-start.16 = (f32[4,1,8,128]{3,2,1,0:T(8,128)S(1)}, f32[4,1,8,128]{3,2,1,0:T(8,128)S(1)}, u32[]{:S(2)}, u32[]{:S(2)}) collective-permute-start(f32[4,1,8,128]{3,2,1,0:T(8,128)S(1)} %get-tuple-element.65), channel_id=1, source_target_pairs={{16,0},{32,16},{48,32},{64,48},{80,64},{96,80},{112,96},{128,112},... | collective-permute-start | bytes 49160 | tf_op jit(solution)/shard_map/ppermute | solution.py:25
  118.6 18.8 %collective-permute-start.18 = (f32[4,4,8,1]{3,2,1,0:T(8,128)S(1)}, f32[4,4,8,1]{3,2,1,0:T(8,128)S(1)}, u32[]{:S(2)}, u32[]{:S(2)}) collective-permute-start(f32[4,4,8,1]{3,2,1,0:T(8,128)S(1)} %get-tuple-element.49), channel_id=1, source_target_pairs={{1,0},{2,1},{3,2},{0,3},{5,4},{6,5},{7,6},{4,7},{9,8},{10,9},{11,1... | collective-permute-start | bytes 1544 | tf_op jit(solution)/shard_map/ppermute | solution.py:25
  122.9 19.8 %collective-permute-start.20 = (f32[4,4,1,128]{3,2,1,0:T(1,128)S(1)}, f32[4,4,1,128]{3,2,1,0:T(1,128)S(1)}, u32[]{:S(2)}, u32[]{:S(2)}) collective-permute-start(f32[4,4,1,128]{3,2,1,0:T(1,128)S(1)} %get-tuple-element.53), channel_id=1, source_target_pairs={{4,0},{8,4},{12,8},{0,12},{5,1},{9,5},{13,9},{1,13},{6,2},{10,6},{... | collective-permute-start | bytes 24584 | tf_op jit(solution)/shard_map/ppermute | solution.py:25
  127.8 14.9 %collective-permute-start.21 = (f32[4,4,1,128]{3,2,1,0:T(1,128)S(1)}, f32[4,4,1,128]{3,2,1,0:T(1,128)S(1)}, u32[]{:S(2)}, u32[]{:S(2)}) collective-permute-start(f32[4,4,1,128]{3,2,1,0:T(1,128)S(1)} %get-tuple-element.54), channel_id=1, source_target_pairs={{0,4},{4,8},{8,12},{12,0},{1,5},{5,9},{9,13},{13,1},{2,6},{6,10},{... | collective-permute-start | bytes 24584 | tf_op jit(solution)/shard_map/ppermute | solution.py:24
  129.7 13.1 %collective-permute-start.22 = (f32[4,1,8,128]{3,2,1,0:T(8,128)S(1)}, f32[4,1,8,128]{3,2,1,0:T(8,128)S(1)}, u32[]{:S(2)}, u32[]{:S(2)}) collective-permute-start(f32[4,1,8,128]{3,2,1,0:T(8,128)S(1)} %get-tuple-element.55), channel_id=1, source_target_pairs={{16,0},{32,16},{48,32},{64,48},{80,64},{96,80},{112,96},{128,112},... | collective-permute-start | bytes 49160 | tf_op jit(solution)/shard_map/ppermute | solution.py:25
  146.9 24.1 %collective-permute-start.26 = (f32[2,4,1,128]{3,2,1,0:T(1,128)}, f32[2,4,1,128]{3,2,1,0:T(1,128)}, u32[]{:S(2)}, u32[]{:S(2)}) collective-permute-start(f32[2,4,1,128]{3,2,1,0:T(1,128)} %get-tuple-element.129), channel_id=1, source_target_pairs={{4,0},{8,4},{12,8},{0,12},{5,1},{9,5},{13,9},{1,13},{6,2},{10,6},{... | collective-permute-start | bytes 12296 | tf_op jit(solution)/shard_map/ppermute | solution.py:25
  151.8 19.2 %collective-permute-start.27 = (f32[2,4,1,128]{3,2,1,0:T(1,128)}, f32[2,4,1,128]{3,2,1,0:T(1,128)}, u32[]{:S(2)}, u32[]{:S(2)}) collective-permute-start(f32[2,4,1,128]{3,2,1,0:T(1,128)} %get-tuple-element.130), channel_id=1, source_target_pairs={{0,4},{4,8},{8,12},{12,0},{1,5},{5,9},{9,13},{13,1},{2,6},{6,10},{... | collective-permute-start | bytes 12296 | tf_op jit(solution)/shard_map/ppermute | solution.py:24
  154.3 17.8 %collective-permute-start.28 = (f32[2,1,8,128]{3,2,1,0:T(8,128)}, f32[2,1,8,128]{3,2,1,0:T(8,128)}, u32[]{:S(2)}, u32[]{:S(2)}) collective-permute-start(f32[2,1,8,128]{3,2,1,0:T(8,128)} %get-tuple-element.133), channel_id=1, source_target_pairs={{16,0},{32,16},{48,32},{64,48},{80,64},{96,80},{112,96},{128,112},... | collective-permute-start | bytes 24584 | tf_op jit(solution)/shard_map/ppermute | solution.py:25
  192.5 19.4 %collective-permute-start.32 = (f32[2,4,1,128]{3,2,1,0:T(1,128)S(1)}, f32[2,4,1,128]{3,2,1,0:T(1,128)S(1)}, u32[]{:S(2)}, u32[]{:S(2)}) collective-permute-start(f32[2,4,1,128]{3,2,1,0:T(1,128)S(1)} %get-tuple-element.117), channel_id=1, source_target_pairs={{4,0},{8,4},{12,8},{0,12},{5,1},{9,5},{13,9},{1,13},{6,2},{10,6},{... | collective-permute-start | bytes 12296 | tf_op jit(solution)/shard_map/ppermute | solution.py:25
  197.4 14.6 %collective-permute-start.33 = (f32[2,4,1,128]{3,2,1,0:T(1,128)S(1)}, f32[2,4,1,128]{3,2,1,0:T(1,128)S(1)}, u32[]{:S(2)}, u32[]{:S(2)}) collective-permute-start(f32[2,4,1,128]{3,2,1,0:T(1,128)S(1)} %get-tuple-element.118), channel_id=1, source_target_pairs={{0,4},{4,8},{8,12},{12,0},{1,5},{5,9},{9,13},{13,1},{2,6},{6,10},{... | collective-permute-start | bytes 12296 | tf_op jit(solution)/shard_map/ppermute | solution.py:24
  230.2 18.9 %collective-permute-start.38 = (f32[2,4,1,128]{3,2,1,0:T(1,128)S(1)}, f32[2,4,1,128]{3,2,1,0:T(1,128)S(1)}, u32[]{:S(2)}, u32[]{:S(2)}) collective-permute-start(f32[2,4,1,128]{3,2,1,0:T(1,128)S(1)} %get-tuple-element.105), channel_id=1, source_target_pairs={{4,0},{8,4},{12,8},{0,12},{5,1},{9,5},{13,9},{1,13},{6,2},{10,6},{... | collective-permute-start | bytes 12296 | tf_op jit(solution)/shard_map/ppermute | solution.py:25
  234.8 14.4 %collective-permute-start.39 = (f32[2,4,1,128]{3,2,1,0:T(1,128)S(1)}, f32[2,4,1,128]{3,2,1,0:T(1,128)S(1)}, u32[]{:S(2)}, u32[]{:S(2)}) collective-permute-start(f32[2,4,1,128]{3,2,1,0:T(1,128)S(1)} %get-tuple-element.106), channel_id=1, source_target_pairs={{0,4},{4,8},{8,12},{12,0},{1,5},{5,9},{9,13},{13,1},{2,6},{6,10},{... | collective-permute-start | bytes 12296 | tf_op jit(solution)/shard_map/ppermute | solution.py:24
  267.7 18.9 %collective-permute-start.44 = (f32[2,4,1,128]{3,2,1,0:T(1,128)S(1)}, f32[2,4,1,128]{3,2,1,0:T(1,128)S(1)}, u32[]{:S(2)}, u32[]{:S(2)}) collective-permute-start(f32[2,4,1,128]{3,2,1,0:T(1,128)S(1)} %get-tuple-element.93), channel_id=1, source_target_pairs={{4,0},{8,4},{12,8},{0,12},{5,1},{9,5},{13,9},{1,13},{6,2},{10,6},{... | collective-permute-start | bytes 12296 | tf_op jit(solution)/shard_map/ppermute | solution.py:25
  272.3 14.4 %collective-permute-start.45 = (f32[2,4,1,128]{3,2,1,0:T(1,128)S(1)}, f32[2,4,1,128]{3,2,1,0:T(1,128)S(1)}, u32[]{:S(2)}, u32[]{:S(2)}) collective-permute-start(f32[2,4,1,128]{3,2,1,0:T(1,128)S(1)} %get-tuple-element.94), channel_id=1, source_target_pairs={{0,4},{4,8},{8,12},{12,0},{1,5},{5,9},{9,13},{13,1},{2,6},{6,10},{... | collective-permute-start | bytes 12296 | tf_op jit(solution)/shard_map/ppermute | solution.py:24
  (203 other events, 3013.5 us)
Sparse Core Ops, SparseCore 0:
  303.5 500.5 all-reduce.2
